TPU v7x, 32 devices: a whole 2x2x4 slice. The times are simulated.
32 devices in a mesh: segment: 8 (over z, y), band: 4 (over x, core).
Axes of the slice: x: 2, y: 2, z: 4, core: 2. Of those that a mesh axis runs over, the one named last changes fastest.
Arguments:
- forward_state: bfloat16 [8, 2, 32, 64, 256], P('segment', None, 'band'), may hold values from -6 to 6
- returning_state: bfloat16 [8, 2, 32, 64, 256], P('segment', None, 'band'), may hold values from -6 to 6
- returning_grad: bfloat16 [8, 2, 32, 64, 256], P('segment', None, 'band'), may hold values from -6 to 6
- weights: bfloat16 [8, 2, 2304, 256], P('segment'), may hold values from -0.125 to 0.125
- fresh_input: bfloat16 [2, 2, 32, 64, 256], P(None, None, 'band'), may hold values from -6 to 6
- loss_grad: bfloat16 [2, 2, 32, 64, 256], P(None, None, 'band'), may hold values from -6 to 6
Outputs:
- forward_out: bfloat16 [8, 2, 32, 64, 256], P('segment', None, 'band')
- returning_out: bfloat16 [8, 2, 32, 64, 256], P('segment', None, 'band')
- backward_out: bfloat16 [8, 2, 32, 64, 256], P('segment', None, 'band')
- weight_grad: float32 [8, 2, 2304, 256], P('segment', None, 'band')
All inputs are finite; a program needn't handle non-finite values.
Results may differ from a plain program's by a relative error of at most 0.02.
Values may be sent and summed in bfloat16 or wider, within the bound.
A program may use at most 64 MiB of HBM per device.

v0:
```python
import functools

import jax
import jax.numpy as jnp
from jax import lax
from jax.experimental import pallas as pl
from jax.experimental.pallas import tpu as pltpu
from jax.sharding import PartitionSpec as P

MESH = pl.DeviceIdType.MESH
ACT_Q, ACT_OUT, ACT_Y, GRAD2, ACT_IN, BACK1 = range(6)
FWD1, FWD2, RET1, RET2, GRD1, GRD2 = range(6)


def kernel(ticks, segments, bands, width, fwd_in, ret_in, grd_in, weights_in, fresh_in, loss_in,
           fwd_out, ret_out, grd_out, wgrad_out,
           fwd_v, ret_v, grd_v, wts, flipped, stack, halo_src, halo_dst, sent, came, total, total_half, paired, reduced, partial,
           in_sem, edge_sem, halo_send, halo_recv, move_send, move_recv, pair_send, pair_recv,
           red_send, red_recv):
    seg = lax.axis_index("segment")
    band = lax.axis_index("band")
    pixels = fwd_v.shape[1]
    channels = fwd_v.shape[2]
    triple = 3 * channels
    chunk = partial.shape[2]
    first_seg, last_seg = seg == 0, seg == segments - 1

    loads = [
        pltpu.make_async_copy(fwd_in, fwd_v, in_sem.at[0]),
        pltpu.make_async_copy(ret_in, ret_v, in_sem.at[1]),
        pltpu.make_async_copy(grd_in, grd_v, in_sem.at[2]),
        pltpu.make_async_copy(weights_in.at[0], wts.at[0], in_sem.at[3]),
        pltpu.make_async_copy(weights_in.at[1], wts.at[1], in_sem.at[4]),
    ]
    for load in loads:
        load.start()

    barrier = pltpu.get_barrier_semaphore()
    for step in range(1, bands):
        pl.semaphore_signal(barrier, inc=1, device_id=(seg, lax.rem(band + step, bands)), device_id_type=MESH)

    @pl.when(seg > 0)
    def _():
        pl.semaphore_signal(barrier, inc=1, device_id=(seg - 1, band), device_id_type=MESH)

    @pl.when(seg < segments - 1)
    def _():
        pl.semaphore_signal(barrier, inc=1, device_id=(seg + 1, band), device_id_type=MESH)

    def landing(tick, field):
        if tick < ticks - 1:
            return came.at[tick, field]
        return (fwd_out, ret_out, grd_out)[field // 2].at[field % 2]

    def edge_copies(tick):
        if tick < ticks - 1:
            targets = (came.at[tick, pl.ds(FWD1, 2)], came.at[tick, pl.ds(GRD1, 2)])
        else:
            targets = (fwd_out, grd_out)
        return (
            pltpu.make_async_copy(fresh_in.at[tick], targets[0], edge_sem.at[tick, 0]),
            pltpu.make_async_copy(loss_in.at[tick], targets[1], edge_sem.at[tick, 1]),
        )

    for tick in range(ticks):
        fresh_copy, loss_copy = edge_copies(tick)
        pl.when(first_seg)(fresh_copy.start)
        pl.when(last_seg)(loss_copy.start)

    column = lax.rem(lax.broadcasted_iota(jnp.int32, (pixels, channels), 0), width)
    at_left, at_right = column == 0, column == width - 1

    def fill(field, start, value):
        rows = value.shape[0]
        wide = value.astype(jnp.float32)
        left = jnp.where(at_left[:rows], 0.0, pltpu.roll(wide, 1, 0))
        right = jnp.where(at_right[:rows], 0.0, pltpu.roll(wide, rows - 1, 0))
        stack[field, start:start + rows, 0:channels] = left.astype(jnp.bfloat16)
        stack[field, start:start + rows, channels:2 * channels] = value
        stack[field, start:start + rows, 2 * channels:triple] = right.astype(jnp.bfloat16)

    def halo_copy(tick, field, side):
        return pltpu.make_async_remote_copy(
            src_ref=halo_src.at[tick, field, side], dst_ref=halo_dst.at[tick, field, 1 - side],
            send_sem=halo_send.at[tick, field, side], recv_sem=halo_recv.at[tick, field, 1 - side],
            device_id=(seg, band - 1 if side == 0 else band + 1), device_id_type=MESH)

    def send_halo(tick, field):
        pl.when(band > 0)(halo_copy(tick, field, 0).start)
        pl.when(band < bands - 1)(halo_copy(tick, field, 1).start)

    def take_halo(tick, field):
        zero = jnp.zeros((width, triple), jnp.bfloat16)

        @pl.when(band > 0)
        def _():
            halo_copy(tick, field, 1).wait_recv()
            fill(field, 0, halo_dst[tick, field, 0])

        @pl.when(band == 0)
        def _():
            stack[field, 0:width] = zero

        @pl.when(band < bands - 1)
        def _():
            halo_copy(tick, field, 0).wait_recv()
            fill(field, pixels + width, halo_dst[tick, field, 1])

        @pl.when(band == bands - 1)
        def _():
            stack[field, pixels + width:pixels + 2 * width] = zero

    def apply(field, kernel_ref):
        result = None
        for row in range(3):
            term = jnp.dot(stack[field, row * width:row * width + pixels],
                           kernel_ref[row * triple:(row + 1) * triple],
                           preferred_element_type=jnp.float32)
            result = term if result is None else result + term
        return result

    def correlate(tick, index, field, grads):
        for row in range(3):
            term = lax.dot_general(stack[field, row * width:row * width + pixels], grads,
                                   (((0,), (0,)), ((), ())), preferred_element_type=jnp.float32)
            rows = slice(row * triple, (row + 1) * triple)
            if tick > 0:
                term = total[index, rows] + term
            total[index, rows] = term
            if tick == ticks - 1:
                total_half[index, rows] = term.astype(jnp.bfloat16)

    def flip(index):
        for tap in range(9):
            back = 8 - tap
            flipped[index, tap * channels:(tap + 1) * channels] = (
                wts[index, back * channels:(back + 1) * channels].T)

    def act(value):
        wide = value.astype(jnp.float32)
        return (wide * jax.nn.sigmoid(wide)).astype(jnp.bfloat16)

    def slope(value):
        wide = value.astype(jnp.float32)
        sigmoid = jax.nn.sigmoid(wide)
        return sigmoid * (1.0 + wide * (1.0 - sigmoid))

    def move_copy(tick, field):
        other = seg + 1 if field < RET1 else seg - 1
        return pltpu.make_async_remote_copy(
            src_ref=sent.at[tick, field], dst_ref=landing(tick, field),
            send_sem=move_send.at[tick, field], recv_sem=move_recv.at[tick, field],
            device_id=(other, band), device_id_type=MESH)

    def send_on(tick, field, value):
        sent[tick, field] = value
        if field < RET1:
            pl.when(seg < segments - 1)(move_copy(tick, field).start)

            @pl.when(last_seg)
            def _():
                landing(tick, field + RET1)[...] = value
        else:
            pl.when(seg > 0)(move_copy(tick, field).start)

    def take(tick, fields):
        for field in fields:
            if field < RET1:
                pl.when(seg > 0)(move_copy(tick, field).wait_recv)
            else:
                pl.when(seg < segments - 1)(move_copy(tick, field).wait_recv)
        fresh_copy, loss_copy = edge_copies(tick)
        if FWD1 in fields:
            pl.when(first_seg)(fresh_copy.wait)
        if GRD1 in fields:
            pl.when(last_seg)(loss_copy.wait)

    groups = bands // 2
    core, group = lax.rem(band, 2), band // 2

    def chunk_rows(owner):
        return pl.ds(pl.multiple_of(owner * chunk, chunk), chunk)

    def pair_copy(index, target):
        return pltpu.make_async_remote_copy(
            src_ref=total_half.at[index, chunk_rows(2 * target + 1 - core)], dst_ref=paired.at[index, target],
            send_sem=pair_send.at[index, target], recv_sem=pair_recv.at[index, target],
            device_id=(seg, band + 1 - 2 * core), device_id_type=MESH)

    def reduce_copy(index, step):
        other = 2 * lax.rem(group + step, groups) + core
        return pltpu.make_async_remote_copy(
            src_ref=reduced.at[index, step - 1], dst_ref=partial.at[index, step - 1],
            send_sem=red_send.at[index, step - 1], recv_sem=red_recv.at[index, step - 1],
            device_id=(seg, other), device_id_type=MESH)

    def start_sums(index):
        for target in range(groups):
            pair_copy(index, target).start()

    def pair_sum(index, target):
        return total[index, chunk_rows(2 * target + core)] + paired[index, target].astype(jnp.float32)

    def pass_sums(index):
        for target in range(groups):
            pair_copy(index, target).wait_recv()
        for step in range(1, groups):
            reduced[index, step - 1] = pair_sum(index, lax.rem(group + step, groups)).astype(jnp.bfloat16)
            reduce_copy(index, step).start()

    def finish_sums(index):
        value = pair_sum(index, group)
        for step in range(1, groups):
            reduce_copy(index, step).wait_recv()
            value = value + partial[index, step - 1].astype(jnp.float32)
        wgrad_out[index] = value

    def begin(tick, field, ref, function):
        halo_src[tick, field, 0] = function(ref[0:width])
        halo_src[tick, field, 1] = function(ref[pixels - width:pixels])
        send_halo(tick, field)
        fill(field, width, function(ref[...]))

    for tick in range(ticks):
        last_tick = tick == ticks - 1
        if tick == 0:
            p, q = fwd_v.at[0], fwd_v.at[1]
            y1, y2 = ret_v.at[0], ret_v.at[1]
            g1, g2 = grd_v.at[0], grd_v.at[1]
        else:
            p, q, y1, y2, g1, g2 = (came.at[tick - 1, field] for field in range(6))

        def same(value):
            return value

        def advance_first():
            take_halo(tick, ACT_Q)
            out1 = (p[...].astype(jnp.float32) + apply(ACT_Q, wts.at[0])).astype(jnp.bfloat16)
            send_on(tick, FWD1, out1)
            begin(tick, ACT_OUT, sent.at[tick, FWD1], act)

        def advance_second():
            take_halo(tick, ACT_OUT)
            out2 = (q[...].astype(jnp.float32) + apply(ACT_OUT, wts.at[1])).astype(jnp.bfloat16)
            send_on(tick, FWD2, out2)

        def invert_second():
            take_halo(tick, ACT_Y)
            q2 = (y2[...].astype(jnp.float32) - apply(ACT_Y, wts.at[1])).astype(jnp.bfloat16)
            send_on(tick, RET2, q2)
            begin(tick, ACT_IN, sent.at[tick, RET2], act)

        def invert_first():
            take_halo(tick, ACT_IN)
            p2 = (y1[...].astype(jnp.float32) - apply(ACT_IN, wts.at[0])).astype(jnp.bfloat16)
            send_on(tick, RET1, p2)

        def back_first():
            take_halo(tick, GRAD2)
            h1 = (g1[...].astype(jnp.float32) + slope(y1[...]) * apply(GRAD2, flipped.at[1])).astype(jnp.bfloat16)
            send_on(tick, GRD1, h1)
            begin(tick, BACK1, sent.at[tick, GRD1], same)

        def back_second():
            take_halo(tick, BACK1)
            h2 = (g2[...].astype(jnp.float32)
                  + slope(sent[tick, RET2]) * apply(BACK1, flipped.at[0])).astype(jnp.bfloat16)
            send_on(tick, GRD2, h2)

        if tick == 0:
            loads[0].wait()
            others = (seg > 0).astype(jnp.int32) + (seg < segments - 1).astype(jnp.int32)
            pl.semaphore_wait(barrier, bands - 1 + others)
            begin(tick, ACT_Q, q, act)
            loads[1].wait()
            begin(tick, ACT_Y, y1, act)
            loads[3].wait()
            advance_first()
            loads[2].wait()
            begin(tick, GRAD2, g2, same)
            loads[4].wait()
            invert_second()
            advance_second()
            flip(1)
            back_first()
            invert_first()
            flip(0)
            back_second()
        else:
            take(tick - 1, (FWD1, FWD2))
            begin(tick, ACT_Q, q, act)
            advance_first()
            advance_second()
            take(tick - 1, (RET1, RET2, GRD1, GRD2))
            begin(tick, ACT_Y, y1, act)
            begin(tick, GRAD2, g2, same)
            invert_second()
            back_first()
        correlate(tick, 1, ACT_Y, g2[...])
        if last_tick:
            start_sums(1)
        if tick > 0:
            invert_first()
        correlate(tick, 0, ACT_IN, sent[tick, GRD1])
        if last_tick:
            start_sums(0)
        if tick > 0:
            back_second()
        if last_tick:
            pass_sums(1)
            pass_sums(0)

    finish_sums(1)
    finish_sums(0)
    take(ticks - 1, range(6))
    for index in range(2):
        for target in range(groups):
            pair_copy(index, target).wait_send()
        for step in range(1, groups):
            reduce_copy(index, step).wait_send()
    for tick in range(ticks):
        for field in range(6):
            pl.when(band > 0)(halo_copy(tick, field, 0).wait_send)
            pl.when(band < bands - 1)(halo_copy(tick, field, 1).wait_send)
            if field < RET1:
                pl.when(seg < segments - 1)(move_copy(tick, field).wait_send)
            else:
                pl.when(seg > 0)(move_copy(tick, field).wait_send)


def store(*refs):
    count = (len(refs) - 2) // 3
    sources, targets, held = refs[:count], refs[count:2 * count], refs[2 * count:3 * count]
    load_sem, store_sem = refs[3 * count:]
    loads = [pltpu.make_async_copy(sources[i], held[i], load_sem.at[i]) for i in range(count)]
    stores = [pltpu.make_async_copy(held[i], targets[i], store_sem.at[i]) for i in range(count)]
    for load in loads:
        load.start()
    for load, out in zip(loads, stores):
        load.wait()
        out.start()
    for out in stores:
        out.wait()


def local(forward_state, returning_state, returning_grad, weights, fresh_input, loss_grad):
    segments, bands = lax.axis_size("segment"), lax.axis_size("band")
    _, _, rows, width, channels = forward_state.shape
    pixels = rows * width
    ticks = fresh_input.shape[0]
    taps = weights.shape[2]
    chunk = taps // bands
    bf16, f32 = jnp.bfloat16, jnp.float32
    pair = jax.ShapeDtypeStruct((2, pixels, channels), bf16)
    dma = pltpu.SemaphoreType.DMA
    flat = lambda x: x.reshape(x.shape[:-3] + (pixels, channels))
    vmem = pl.BlockSpec(memory_space=pltpu.VMEM)
    outs = pl.pallas_call(
        functools.partial(kernel, ticks, segments, bands, width),
        out_shape=(pair, pair, pair, jax.ShapeDtypeStruct((2, chunk, channels), f32)),
        in_specs=[pl.BlockSpec(memory_space=pl.ANY)] * 6,
        out_specs=(vmem,) * 4,
        scratch_shapes=[
            pltpu.VMEM((2, pixels, channels), bf16),
            pltpu.VMEM((2, pixels, channels), bf16),
            pltpu.VMEM((2, pixels, channels), bf16),
            pltpu.VMEM((2, taps, channels), bf16),
            pltpu.VMEM((2, taps, channels), bf16),
            pltpu.VMEM((6, pixels + 2 * width, 3 * channels), bf16),
            pltpu.VMEM((ticks, 6, 2, width, channels), bf16),
            pltpu.VMEM((ticks, 6, 2, width, channels), bf16),
            pltpu.VMEM((ticks, 6, pixels, channels), bf16),
            pltpu.VMEM((max(ticks - 1, 1), 6, pixels, channels), bf16),
            pltpu.VMEM((2, taps, channels), f32),
            pltpu.VMEM((2, taps, channels), bf16),
            pltpu.VMEM((2, bands // 2, chunk, channels), bf16),
            pltpu.VMEM((2, bands // 2 - 1, chunk, channels), bf16),
            pltpu.VMEM((2, bands // 2 - 1, chunk, channels), bf16),
            dma((5,)),
            dma((ticks, 2)),
            dma((ticks, 6, 2)),
            dma((ticks, 6, 2)),
            dma((ticks, 6)),
            dma((ticks, 6)),
            dma((2, bands // 2)),
            dma((2, bands // 2)),
            dma((2, bands // 2 - 1)),
            dma((2, bands // 2 - 1)),
        ],
        compiler_params=pltpu.CompilerParams(
            collective_id=0, has_side_effects=True, vmem_limit_bytes=60 * 2**20),
    )(flat(forward_state[0]), flat(returning_state[0]), flat(returning_grad[0]), weights[0],
      flat(fresh_input), flat(loss_grad))
    outs = pl.pallas_call(
        store,
        out_shape=tuple(jax.ShapeDtypeStruct(o.shape, o.dtype) for o in outs),
        in_specs=[pl.BlockSpec(memory_space=pl.ANY)] * 4,
        out_specs=(pl.BlockSpec(memory_space=pl.ANY),) * 4,
        scratch_shapes=[pltpu.VMEM(o.shape, o.dtype) for o in outs] + [dma((4,)), dma((4,))],
    )(*outs)
    shape = forward_state.shape
    return tuple(o.reshape(shape) for o in outs[:3]) + (outs[3][None],)


def solution(mesh):
    pair = P("segment", None, "band", None, None)
    whole = P(None, None, "band", None, None)
    return jax.shard_map(
        local,
        mesh=mesh,
        in_specs=(pair, pair, pair, P("segment", None, None, None), whole, whole),
        out_specs=(pair, pair, pair, P("segment", None, "band", None)),
        check_vma=False,
    )
```

profile of v0, /device:TPU:17, one launch (start us, length us, event | category | flops | bytes accessed | tf_op | source)
XLA Modules:
  0.0 86.4 jit_solution(5520058149305290481)
XLA Ops:
  0.6 82.7 %shard_map.93 = (bf16[2,512,256]{2,1,0:T(8,128)(2,1)}, bf16[2,512,256]{2,1,0:T(8,128)(2,1)}, bf16[2,512,256]{2,1,0:T(8,128)(2,1)}, f32[2,576,256]{2,1,0:T(8,128)}) custom-call(bf16[2,512,256]{2,1,0:T(8,128)(2,1)} %bitcast.13, bf16[2,512,256]{2,1,0:T(8,128)(2,1)} %bitcast.14, bf16[2,512,256]{2,1,0:T(8,128)(2,1)} %bitcast.15, bf16[2,2304,256]{2,1,0:T(8,128)(2,1)} %bitcast.10, ...), custom_call_target="tpu_custom_call" | custom-call | tf_op jit(solution)/shard_map/pallas_call | solution.py:358
  83.4 2.8 %shard_map.94 = (bf16[2,512,256]{2,1,0:T(8,128)(2,1)}, bf16[2,512,256]{2,1,0:T(8,128)(2,1)}, bf16[2,512,256]{2,1,0:T(8,128)(2,1)}, f32[2,576,256]{2,1,0:T(8,128)}) custom-call(bf16[2,512,256]{2,1,0:T(8,128)(2,1)} %get-tuple-element.12.refs_0_, bf16[2,512,256]{2,1,0:T(8,128)(2,1)} %get-tuple-element.13.refs_1_, ...), custom_call_target="tpu_custom_call" | custom-call | tf_op jit(solution)/shard_map/pallas_call | solution.py:394
where the time goes:
time: 86.5 us; the launch traced here: 86.4 us
  Pallas kernels  85.6 us (99%)
    pallas_call x1, Pallas kernels, local(): pl.pallas_call(functools.partial(kernel, ticks, segments, bands, width),...  82.7 us
    pallas_call x1, Pallas kernels, local(): pl.pallas_call(store, out_shape=tuple((jax.ShapeDtypeStruct(o.shape, o.dt...  2.84 us

commit v1 on v0

v1 whole, which is shorter than its diff:
```python
import functools

import jax
import jax.numpy as jnp
from jax import lax
from jax.experimental import pallas as pl
from jax.experimental.pallas import tpu as pltpu
from jax.sharding import PartitionSpec as P

MESH = pl.DeviceIdType.MESH
ACT_Q, ACT_OUT, ACT_Y, GRAD2, ACT_IN, BACK1 = range(6)
FWD1, FWD2, RET1, RET2, GRD1, GRD2 = range(6)
F, G = 0, 1
OWN, OTHER = 0, 1
DEPTH = {FWD1: 1, FWD2: 2, RET1: 2, RET2: 1, GRD1: 1, GRD2: 2}


def kernel(segments, bands, width, pieces, fwd_in, ret_in, grd_in, weights_in, fresh_in, loss_in,
           fwd_out, ret_out, grd_out, wgrad_out,
           fields, wts, stack, sent, total, total_half, paired, reduced, partial, owned, ship_src, ship_dst,
           in_sem, w_sem, edge_sem, halo_send, halo_recv, mid_send, mid_recv, end_send, end_recv,
           wy_send, wy_recv, wx_send, wx_recv, wc_send, wc_recv,
           pair_send, pair_recv, red_send, red_recv, ship_send, ship_recv):
    seg = lax.axis_index("segment")
    band = lax.axis_index("band")
    pixels = sent.shape[2]
    channels = sent.shape[3]
    triple = 3 * channels
    chunk = partial.shape[3]
    margin = 2 * width
    inner = pl.ds(margin, pixels)
    first_pixels = pixels + 2 * width
    parity = lax.rem(seg, 2)
    even, odd = parity == 0, parity == 1
    other_seg = seg + 1 - 2 * parity
    first_seg, last_seg = seg == 0, seg == segments - 1
    below, above = seg >= 2, seg < segments - 2
    groups = bands // 2
    core, group = lax.rem(band, 2), band // 2
    core_band = band + 1 - 2 * core
    at_top, at_bottom = band == 0, band == bands - 1

    sources = {FWD1: fwd_in.at[0], FWD2: fwd_in.at[1], RET1: ret_in.at[0], RET2: ret_in.at[1],
               GRD1: grd_in.at[0], GRD2: grd_in.at[1]}

    def load(field):
        return pltpu.make_async_copy(sources[field], fields.at[0, field, inner], in_sem.at[field])

    def load_weights(index):
        return pltpu.make_async_copy(weights_in.at[index], wts.at[OWN, index], w_sem.at[index])

    load(RET1).start()
    load(GRD2).start()
    load_weights(G).start()
    load(RET2).start()
    load(GRD1).start()
    load_weights(F).start()
    load(FWD2).start()
    load(FWD1).start()

    barrier = pltpu.get_barrier_semaphore()
    for step in range(1, bands):
        pl.semaphore_signal(barrier, inc=1, device_id=(seg, lax.rem(band + step, bands)), device_id_type=MESH)
    pl.semaphore_signal(barrier, inc=1, device_id=(other_seg, band), device_id_type=MESH)

    @pl.when(below)
    def _():
        pl.semaphore_signal(barrier, inc=1, device_id=(seg - 2, band), device_id_type=MESH)

    @pl.when(above)
    def _():
        pl.semaphore_signal(barrier, inc=1, device_id=(seg + 2, band), device_id_type=MESH)

    def edge(which):
        return (
            pltpu.make_async_copy(fresh_in.at[0], fields.at[1, pl.ds(FWD1, 2), inner], edge_sem.at[0]),
            pltpu.make_async_copy(fresh_in.at[1], fwd_out, edge_sem.at[1]),
            pltpu.make_async_copy(loss_in.at[0], fields.at[1, pl.ds(GRD1, 2), inner], edge_sem.at[2]),
            pltpu.make_async_copy(loss_in.at[1], grd_out, edge_sem.at[3]),
        )[which]

    edge_places = (seg == 1, first_seg, seg == segments - 2, last_seg)
    for which in range(4):
        pl.when(edge_places[which])(edge(which).start)

    @pl.when(at_top)
    def _():
        fields[:, :, 0:margin] = jnp.zeros((2, 6, margin, channels), jnp.bfloat16)

    @pl.when(at_bottom)
    def _():
        fields[:, :, margin + pixels:] = jnp.zeros((2, 6, margin, channels), jnp.bfloat16)

    def halo_copy(tick, field, side):
        size = DEPTH[field] * width
        if side == 0:
            source, target = margin, margin + pixels
        else:
            source, target = margin + pixels - size, margin - size
        return pltpu.make_async_remote_copy(
            src_ref=fields.at[tick, field, pl.ds(source, size)], dst_ref=fields.at[tick, field, pl.ds(target, size)],
            send_sem=halo_send.at[tick, field, side], recv_sem=halo_recv.at[tick, field, 1 - side],
            device_id=(seg, band - 1 if side == 0 else band + 1), device_id_type=MESH)

    def send_halo(tick, field):
        pl.when(jnp.logical_not(at_top))(halo_copy(tick, field, 0).start)
        pl.when(jnp.logical_not(at_bottom))(halo_copy(tick, field, 1).start)

    def take_halo(tick, field):
        pl.when(jnp.logical_not(at_top))(halo_copy(tick, field, 1).wait_recv)
        pl.when(jnp.logical_not(at_bottom))(halo_copy(tick, field, 0).wait_recv)

    piece = chunk // pieces

    def w_rows(owner, part):
        return pl.ds(pl.multiple_of(owner * chunk + part * piece, piece), piece)

    def w_across(index, part):
        return pltpu.make_async_remote_copy(
            src_ref=wts.at[OWN, index, w_rows(band, part)], dst_ref=wts.at[OTHER, index, w_rows(band, part)],
            send_sem=wy_send.at[index, part], recv_sem=wy_recv.at[index, part],
            device_id=(other_seg, band), device_id_type=MESH)

    def w_group(index, part, step):
        rows = w_rows(band, part)
        return pltpu.make_async_remote_copy(
            src_ref=wts.at[OTHER, index, rows], dst_ref=wts.at[OTHER, index, rows],
            send_sem=wx_send.at[index, part, step - 1], recv_sem=wx_recv.at[index, part, step - 1],
            device_id=(seg, 2 * lax.rem(group + step, groups) + core), device_id_type=MESH)

    def w_core(index, part, step):
        rows = w_rows(2 * lax.rem(group + groups - step, groups) + core, part)
        return pltpu.make_async_remote_copy(
            src_ref=wts.at[OTHER, index, rows], dst_ref=wts.at[OTHER, index, rows],
            send_sem=wc_send.at[index, part, step], recv_sem=wc_recv.at[index, part, step],
            device_id=(seg, core_band), device_id_type=MESH)

    def spread_weights(index, part):
        w_across(index, part).wait_recv()
        for step in range(1, groups):
            w_group(index, part, step).start()
        w_core(index, part, 0).start()

    def pass_weights(index, part):
        for step in range(1, groups):
            w_group(index, part, step).wait_recv()
            w_core(index, part, step).start()

    def take_weights(index):
        for part in range(pieces):
            for step in range(groups):
                w_core(index, part, step).wait_recv()

    def fill(slot, value):
        rows = value.shape[0]
        column = lax.rem(lax.broadcasted_iota(jnp.int32, (rows, channels), 0), width)
        wide = value.astype(jnp.float32)
        left = jnp.where(column == 0, 0.0, pltpu.roll(wide, 1, 0))
        right = jnp.where(column == width - 1, 0.0, pltpu.roll(wide, rows - 1, 0))
        stack[slot, 0:rows, 0:channels] = left.astype(jnp.bfloat16)
        stack[slot, 0:rows, channels:2 * channels] = value
        stack[slot, 0:rows, 2 * channels:triple] = right.astype(jnp.bfloat16)

    def conv(slot, weight, rows):
        result = None
        for row in range(3):
            term = jnp.dot(stack[slot, row * width:row * width + rows], weight[row * triple:(row + 1) * triple],
                           preferred_element_type=jnp.float32)
            result = term if result is None else result + term
        return result

    def back(slot, weight, rows):
        result = None
        for tap in range(9):
            row, col = tap // 3, tap % 3
            start = (8 - tap) * channels
            term = lax.dot_general(stack[slot, row * width:row * width + rows, col * channels:(col + 1) * channels],
                                   weight[start:start + channels], (((1,), (1,)), ((), ())),
                                   preferred_element_type=jnp.float32)
            result = term if result is None else result + term
        return result

    def correlate(which, index, slot, offset, grads):
        for row in range(3):
            start = offset + row * width
            term = lax.dot_general(stack[slot, start:start + pixels], grads, (((0,), (0,)), ((), ())),
                                   preferred_element_type=jnp.float32)
            rows = slice(row * triple, (row + 1) * triple)
            total[which, index, rows] = term
            total_half[which, index, rows] = term.astype(jnp.bfloat16)

    def act(value):
        wide = value.astype(jnp.float32)
        return (wide * jax.nn.sigmoid(wide)).astype(jnp.bfloat16)

    def slope(value):
        wide = value.astype(jnp.float32)
        sigmoid = jax.nn.sigmoid(wide)
        return sigmoid * (1.0 + wide * (1.0 - sigmoid))

    place = lax.broadcasted_iota(jnp.int32, (first_pixels, channels), 0)
    inside = jnp.logical_and(place >= jnp.where(at_top, width, 0),
                             place < jnp.where(at_bottom, width + pixels, first_pixels))

    def trim(value):
        return jnp.where(inside, value, 0.0).astype(jnp.bfloat16)

    grown = slice(width, margin + pixels + width)
    core_rows = slice(margin, margin + pixels)
    kept = slice(width, width + pixels)

    class Tick:
        def __init__(self, tick, which, put, got):
            self.tick, self.which, self.put, self.got = tick, which, put, got

        def field(self, name, rows=core_rows):
            return fields[self.tick, name, rows]

        def weight(self, index):
            return wts.at[self.which, index]

        def advance_first(self):
            fill(ACT_Q, act(fields[self.tick, FWD2]))
            out1 = trim(self.field(FWD1, grown).astype(jnp.float32) + conv(ACT_Q, self.weight(F), first_pixels))
            self.put(FWD1, out1[kept])
            fill(ACT_OUT, act(out1))

        def advance_second(self):
            out2 = self.field(FWD2).astype(jnp.float32) + conv(ACT_OUT, self.weight(G), pixels)
            self.put(FWD2, out2.astype(jnp.bfloat16))

        def fill_returning(self):
            fill(ACT_Y, act(fields[self.tick, RET1]))

        def fill_grad(self):
            fill(GRAD2, fields[self.tick, GRD2])

        def invert_second(self):
            q2 = trim(self.field(RET2, grown).astype(jnp.float32) - conv(ACT_Y, self.weight(G), first_pixels))
            self.put(RET2, q2[kept])
            fill(ACT_IN, act(q2))

        def back_first(self):
            h1 = trim(self.field(GRD1, grown).astype(jnp.float32)
                      + slope(self.field(RET1, grown)) * back(GRAD2, self.weight(G), first_pixels))
            self.put(GRD1, h1[kept])
            fill(BACK1, h1)

        def invert_first(self):
            p2 = self.field(RET1).astype(jnp.float32) - conv(ACT_IN, self.weight(F), pixels)
            self.put(RET1, p2.astype(jnp.bfloat16))

        def back_second(self):
            h2 = (self.field(GRD2).astype(jnp.float32)
                  + slope(self.got(RET2)) * back(BACK1, self.weight(F), pixels))
            self.put(GRD2, h2.astype(jnp.bfloat16))

        def correlate_g(self):
            correlate(self.tick, G, ACT_Y, width, self.field(GRD2))

        def correlate_f(self):
            correlate(self.tick, F, ACT_IN, 0, self.got(GRD1))

    def move(tick, field, target, device):
        return pltpu.make_async_remote_copy(
            src_ref=sent.at[tick, field], dst_ref=target[0], send_sem=(mid_send, end_send)[tick].at[field],
            recv_sem=(mid_recv, end_recv)[tick].at[target[1]], device_id=(device, band), device_id_type=MESH)

    def mid_target(field):
        return fields.at[1, field, inner], field

    def end_target(field):
        return (fwd_out, ret_out, grd_out)[field // 2].at[field % 2], field

    def mid_move(field):
        return move(0, field, mid_target(field), seg + 2 if field < RET1 else seg - 2)

    def turn_move(field):
        return move(0, field, mid_target(field + 2), seg - 1)

    def end_move(field):
        return move(1, field, end_target(field), seg + 2 if field < RET1 else seg - 2)

    def leave_move(field):
        return move(1, field, end_target(field + 2), seg + 1)

    mid_back = jnp.logical_and(even, below)
    mid_on = jnp.logical_and(odd, above)
    end_on = jnp.logical_and(even, above)
    end_back = jnp.logical_and(odd, below)
    leaves = seg == segments - 2

    def send_mid(field):
        if field < RET1:
            pl.when(mid_on)(mid_move(field).start)
            pl.when(last_seg)(turn_move(field).start)
        else:
            pl.when(mid_back)(mid_move(field).start)

    def put_mid(field, value):
        sent[0, field] = value
        if field != GRD1:
            send_mid(field)

        @pl.when(even if field < RET1 else odd)
        def _():
            fields[1, field, core_rows] = value

    def chunk_rows(owner):
        return pl.ds(pl.multiple_of(owner * chunk, chunk), chunk)

    def pair_copy(which, index, target):
        return pltpu.make_async_remote_copy(
            src_ref=total_half.at[which, index, chunk_rows(2 * target + 1 - core)],
            dst_ref=paired.at[which, index, target],
            send_sem=pair_send.at[which, index, target], recv_sem=pair_recv.at[which, index, target],
            device_id=(seg, core_band), device_id_type=MESH)

    def reduce_copy(which, index, step):
        return pltpu.make_async_remote_copy(
            src_ref=reduced.at[which, index, step - 1], dst_ref=partial.at[which, index, step - 1],
            send_sem=red_send.at[which, index, step - 1], recv_sem=red_recv.at[which, index, step - 1],
            device_id=(seg, 2 * lax.rem(group + step, groups) + core), device_id_type=MESH)

    def ship_copy(index):
        return pltpu.make_async_remote_copy(
            src_ref=ship_src.at[index], dst_ref=ship_dst.at[index],
            send_sem=ship_send.at[index], recv_sem=ship_recv.at[index],
            device_id=(other_seg, band), device_id_type=MESH)

    def start_sums(which, index):
        for target in range(groups):
            pair_copy(which, index, target).start()

    def pair_sum(which, index, target):
        return total[which, index, chunk_rows(2 * target + core)] + paired[which, index, target].astype(jnp.float32)

    def pass_sums(which, index):
        for target in range(groups):
            pair_copy(which, index, target).wait_recv()
        for step in range(1, groups):
            reduced[which, index, step - 1] = pair_sum(which, index, lax.rem(group + step, groups)).astype(jnp.bfloat16)
            reduce_copy(which, index, step).start()

    def finish_sums(which, index):
        value = pair_sum(which, index, group)
        for step in range(1, groups):
            reduce_copy(which, index, step).wait_recv()
            value = value + partial[which, index, step - 1].astype(jnp.float32)
        return value

    def keep_sums(index):
        owned[index] = finish_sums(OWN, index)

    def ship_sums(index):
        ship_src[index] = finish_sums(OTHER, index).astype(jnp.bfloat16)
        ship_copy(index).start()

    def close_sums(index):
        ship_copy(index).wait_recv()
        wgrad_out[index] = owned[index] + ship_dst[index].astype(jnp.float32)

    first = Tick(0, OWN, put_mid, lambda field: sent[0, field])
    load(RET1).wait()
    load(GRD2).wait()
    load_weights(G).wait()
    load(RET2).wait()
    load(GRD1).wait()
    load_weights(F).wait()
    load(FWD2).wait()
    load(FWD1).wait()
    neighbours = below.astype(jnp.int32) + above.astype(jnp.int32)
    pl.semaphore_wait(barrier, bands + neighbours)
    for field in (RET1, GRD2, RET2, GRD1, FWD2, FWD1):
        send_halo(0, field)
    for index in (G, F):
        for part in range(pieces):
            w_across(index, part).start()

    take_halo(0, RET1)
    first.fill_returning()
    take_halo(0, RET2)
    first.invert_second()
    take_halo(0, GRD2)
    first.fill_grad()
    take_halo(0, GRD1)
    first.back_first()
    first.invert_first()
    first.back_second()
    send_mid(GRD1)

    @pl.when(odd)
    def _():
        for field in (RET1, GRD2, RET2, GRD1):
            send_halo(1, field)

    for part in range(pieces - 1):
        spread_weights(G, part)
    take_halo(0, FWD2)
    take_halo(0, FWD1)
    first.advance_first()
    first.advance_second()

    @pl.when(even)
    def _():
        for field in (FWD2, FWD1):
            send_halo(1, field)

    spread_weights(G, pieces - 1)
    first.correlate_g()
    start_sums(OWN, G)
    first.correlate_f()
    start_sums(OWN, F)
    for part in range(pieces):
        pass_weights(G, part)
    for part in range(pieces - 1):
        spread_weights(F, part)

    @pl.when(odd)
    def _():
        def put(field, value):
            if field < RET1:
                fwd_out[field] = value
            else:
                sent[1, field] = value
                pl.when(end_back)(end_move(field).start)

        last = Tick(1, OTHER, put, lambda field: sent[1, field])
        take_halo(1, RET1)
        last.fill_returning()
        take_halo(1, GRD2)
        last.fill_grad()
        take_halo(1, RET2)
        take_halo(1, GRD1)
        take_weights(G)
        last.invert_second()
        last.back_first()
        last.correlate_g()
        start_sums(OTHER, G)
        last.correlate_f()
        start_sums(OTHER, F)
        spread_weights(F, pieces - 1)
        for part in range(pieces):
            pass_weights(F, part)
        pass_sums(OTHER, G)
        pass_sums(OTHER, F)
        take_weights(F)
        last.invert_first()
        last.back_second()
        pass_sums(OWN, G)
        pass_sums(OWN, F)

        for field in (FWD2, FWD1):
            pl.when(below)(mid_move(field).wait_recv)
        pl.when(seg == 1)(edge(0).wait)
        for field in (FWD2, FWD1):
            send_halo(1, field)
        for field in (FWD2, FWD1):
            take_halo(1, field)
        last.advance_first()
        last.advance_second()
        ship_sums(G)
        ship_sums(F)
        keep_sums(G)
        keep_sums(F)

    @pl.when(even)
    def _():
        def put(field, value):
            if field < RET1:
                sent[1, field] = value
                pl.when(end_on)(end_move(field).start)
                pl.when(leaves)(leave_move(field).start)
            else:
                (ret_out, grd_out)[field // 2 - 1][field % 2] = value

        last = Tick(1, OTHER, put, lambda field: (ret_out, grd_out)[field // 2 - 1][field % 2])
        spread_weights(F, pieces - 1)
        for part in range(pieces):
            pass_weights(F, part)
        pass_sums(OWN, G)
        pass_sums(OWN, F)
        take_weights(F)
        take_weights(G)
        for field in (FWD2, FWD1):
            take_halo(1, field)
        last.advance_first()
        last.advance_second()

        def arrive(field):
            if field < GRD1:
                mid_move(field).wait_recv()
            else:
                pl.when(above)(mid_move(field).wait_recv)
                if field == GRD2:
                    pl.when(leaves)(edge(2).wait)
            send_halo(1, field)

        arrive(RET2)
        arrive(RET1)
        take_halo(1, RET1)
        last.fill_returning()
        take_halo(1, RET2)
        last.invert_second()
        arrive(GRD2)
        keep_sums(G)
        keep_sums(F)
        take_halo(1, GRD2)
        last.correlate_g()
        start_sums(OTHER, G)
        last.fill_grad()
        arrive(GRD1)
        take_halo(1, GRD1)
        pass_sums(OTHER, G)
        last.back_first()
        last.correlate_f()
        start_sums(OTHER, F)
        last.invert_first()
        pass_sums(OTHER, F)
        last.back_second()
        ship_sums(G)
        ship_sums(F)

    close_sums(G)
    close_sums(F)

    pl.when(first_seg)(edge(1).wait)
    pl.when(last_seg)(edge(3).wait)
    for field in (FWD1, FWD2):
        pl.when(jnp.logical_and(even, below))(end_move(field).wait_recv)
        pl.when(last_seg)(end_move(field + 2).wait_recv)
    for field in (RET1, RET2, GRD1, GRD2):
        pl.when(jnp.logical_and(odd, above))(end_move(field).wait_recv)

    for field in range(6):
        for tick in range(2):
            pl.when(jnp.logical_not(at_top))(halo_copy(tick, field, 0).wait_send)
            pl.when(jnp.logical_not(at_bottom))(halo_copy(tick, field, 1).wait_send)
        if field < RET1:
            pl.when(mid_on)(mid_move(field).wait_send)
            pl.when(last_seg)(turn_move(field).wait_send)
            pl.when(end_on)(end_move(field).wait_send)
            pl.when(leaves)(leave_move(field).wait_send)
        else:
            pl.when(mid_back)(mid_move(field).wait_send)
            pl.when(end_back)(end_move(field).wait_send)
    for index in range(2):
        for part in range(pieces):
            w_across(index, part).wait_send()
            for step in range(1, groups):
                w_group(index, part, step).wait_send()
            for step in range(groups):
                w_core(index, part, step).wait_send()
        for which in range(2):
            for target in range(groups):
                pair_copy(which, index, target).wait_send()
            for step in range(1, groups):
                reduce_copy(which, index, step).wait_send()
        ship_copy(index).wait_send()


def store(*refs):
    count = (len(refs) - 2) // 3
    sources, targets, held = refs[:count], refs[count:2 * count], refs[2 * count:3 * count]
    load_sem, store_sem = refs[3 * count:]
    loads = [pltpu.make_async_copy(sources[i], held[i], load_sem.at[i]) for i in range(count)]
    stores = [pltpu.make_async_copy(held[i], targets[i], store_sem.at[i]) for i in range(count)]
    for load in loads:
        load.start()
    for load, out in zip(loads, stores):
        load.wait()
        out.start()
    for out in stores:
        out.wait()


def local(forward_state, returning_state, returning_grad, weights, fresh_input, loss_grad):
    segments, bands = lax.axis_size("segment"), lax.axis_size("band")
    _, _, rows, width, channels = forward_state.shape
    pixels = rows * width
    taps = weights.shape[2]
    chunk = taps // bands
    groups = bands // 2
    pieces = 2 if chunk % 32 == 0 else 1
    assert fresh_input.shape[0] == 2 and segments % 2 == 0 and bands % 2 == 0 and rows >= 2
    bf16, f32 = jnp.bfloat16, jnp.float32
    pair = jax.ShapeDtypeStruct((2, pixels, channels), bf16)
    dma = pltpu.SemaphoreType.DMA
    flat = lambda x: x.reshape(x.shape[:-3] + (pixels, channels))
    vmem = pl.BlockSpec(memory_space=pltpu.VMEM)
    outs = pl.pallas_call(
        functools.partial(kernel, segments, bands, width, pieces),
        out_shape=(pair, pair, pair, jax.ShapeDtypeStruct((2, chunk, channels), f32)),
        in_specs=[pl.BlockSpec(memory_space=pl.ANY)] * 6,
        out_specs=(vmem,) * 4,
        scratch_shapes=[
            pltpu.VMEM((2, 6, pixels + 4 * width, channels), bf16),
            pltpu.VMEM((2, 2, taps, channels), bf16),
            pltpu.VMEM((6, pixels + 4 * width, 3 * channels), bf16),
            pltpu.VMEM((2, 6, pixels, channels), bf16),
            pltpu.VMEM((2, 2, taps, channels), f32),
            pltpu.VMEM((2, 2, taps, channels), bf16),
            pltpu.VMEM((2, 2, groups, chunk, channels), bf16),
            pltpu.VMEM((2, 2, groups - 1, chunk, channels), bf16),
            pltpu.VMEM((2, 2, groups - 1, chunk, channels), bf16),
            pltpu.VMEM((2, chunk, channels), f32),
            pltpu.VMEM((2, chunk, channels), bf16),
            pltpu.VMEM((2, chunk, channels), bf16),
            dma((6,)),
            dma((2,)),
            dma((4,)),
            dma((2, 6, 2)),
            dma((2, 6, 2)),
            dma((6,)),
            dma((6,)),
            dma((6,)),
            dma((6,)),
            dma((2, pieces)),
            dma((2, pieces)),
            dma((2, pieces, groups - 1)),
            dma((2, pieces, groups - 1)),
            dma((2, pieces, groups)),
            dma((2, pieces, groups)),
            dma((2, 2, groups)),
            dma((2, 2, groups)),
            dma((2, 2, groups - 1)),
            dma((2, 2, groups - 1)),
            dma((2,)),
            dma((2,)),
        ],
        compiler_params=pltpu.CompilerParams(
            collective_id=0, has_side_effects=True, vmem_limit_bytes=60 * 2**20),
    )(flat(forward_state[0]), flat(returning_state[0]), flat(returning_grad[0]), weights[0],
      flat(fresh_input), flat(loss_grad))
    outs = pl.pallas_call(
        store,
        out_shape=tuple(jax.ShapeDtypeStruct(o.shape, o.dtype) for o in outs),
        in_specs=[pl.BlockSpec(memory_space=pl.ANY)] * 4,
        out_specs=(pl.BlockSpec(memory_space=pl.ANY),) * 4,
        scratch_shapes=[pltpu.VMEM(o.shape, o.dtype) for o in outs] + [dma((4,)), dma((4,))],
    )(*outs)
    shape = forward_state.shape
    return tuple(o.reshape(shape) for o in outs[:3]) + (outs[3][None],)


def solution(mesh):
    pair = P("segment", None, "band", None, None)
    whole = P(None, None, "band", None, None)
    return jax.shard_map(
        local,
        mesh=mesh,
        in_specs=(pair, pair, pair, P("segment", None, None, None), whole, whole),
        out_specs=(pair, pair, pair, P("segment", None, "band", None)),
        check_vma=False,
    )
```

time: 86.5 us -> 81.5 us (0.942)
  the two profiles are of different devices: /device:TPU:17 before, /device:TPU:1 now
where the time goes in v1:
time: 81.5 us; the launch traced here: 81.3 us
  Pallas kernels  80.5 us (99%)
  between operations  0.82 us (1%)
    pallas_call x1, Pallas kernels, local(): pl.pallas_call(functools.partial(kernel, segments, bands, width, pieces),...  77.6 us
    pallas_call x1, Pallas kernels, local(): pl.pallas_call(store, out_shape=tuple((jax.ShapeDtypeStruct(o.shape, o.dt...  2.84 us

profile of v1, /device:TPU:1, one launch (start us, length us, event | category | flops | bytes accessed | tf_op | source)
XLA Modules:
  0.0 81.3 jit_solution(16427747139536961940)
XLA Ops:
  0.6 77.6 %shard_map.93 = (bf16[2,512,256]{2,1,0:T(8,128)(2,1)}, bf16[2,512,256]{2,1,0:T(8,128)(2,1)}, bf16[2,512,256]{2,1,0:T(8,128)(2,1)}, f32[2,576,256]{2,1,0:T(8,128)}) custom-call(bf16[2,512,256]{2,1,0:T(8,128)(2,1)} %bitcast.13, bf16[2,512,256]{2,1,0:T(8,128)(2,1)} %bitcast.14, bf16[2,512,256]{2,1,0:T(8,128)(2,1)} %bitcast.15, bf16[2,2304,256]{2,1,0:T(8,128)(2,1)} %bitcast.10, ...), custom_call_target="tpu_custom_call" | custom-call | tf_op jit(solution)/shard_map/pallas_call | solution.py:591
  78.3 2.8 %shard_map.94 = (bf16[2,512,256]{2,1,0:T(8,128)(2,1)}, bf16[2,512,256]{2,1,0:T(8,128)(2,1)}, bf16[2,512,256]{2,1,0:T(8,128)(2,1)}, f32[2,576,256]{2,1,0:T(8,128)}) custom-call(bf16[2,512,256]{2,1,0:T(8,128)(2,1)} %get-tuple-element.12.refs_0_, bf16[2,512,256]{2,1,0:T(8,128)(2,1)} %get-tuple-element.13.refs_1_, ...), custom_call_target="tpu_custom_call" | custom-call | tf_op jit(solution)/shard_map/pallas_call | solution.py:635

commit v2 on v1

--- a/solution.py
+++ b/solution.py
@@ -12,6 +12,7 @@
 FWD1, FWD2, RET1, RET2, GRD1, GRD2 = range(6)
 F, G = 0, 1
 OWN, OTHER = 0, 1
+TAKES = {ACT_Q: FWD2, ACT_Y: RET1, GRAD2: GRD2}
 DEPTH = {FWD1: 1, FWD2: 2, RET1: 2, RET2: 1, GRD1: 1, GRD2: 2}
 
 
@@ -135,10 +136,29 @@
             send_sem=wc_send.at[index, part, step], recv_sem=wc_recv.at[index, part, step],
             device_id=(seg, core_band), device_id_type=MESH)
 
+    def w_direct(index, part, step):
+        rows = w_rows(2 * lax.rem(group + groups - step, groups) + core, part)
+        return pltpu.make_async_remote_copy(
+            src_ref=wts.at[OWN, index, rows], dst_ref=wts.at[OTHER, index, rows],
+            send_sem=wx_send.at[index, part, step - 1], recv_sem=wx_recv.at[index, part, step - 1],
+            device_id=(other_seg, band), device_id_type=MESH)
+
+    straight = jnp.logical_and(above, other_seg < segments - 2) if groups == 2 else jnp.bool_(False)
+
+    def start_weights(index):
+        for part in range(pieces):
+            w_across(index, part).start()
+            if index == F:
+                for step in range(1, groups):
+                    pl.when(straight)(w_direct(index, part, step).start)
+
     def spread_weights(index, part):
         w_across(index, part).wait_recv()
         for step in range(1, groups):
-            w_group(index, part, step).start()
+            if index == F:
+                pl.when(jnp.logical_not(straight))(w_group(index, part, step).start)
+            else:
+                w_group(index, part, step).start()
         w_core(index, part, 0).start()
 
     def pass_weights(index, part):
@@ -151,15 +171,15 @@
             for step in range(groups):
                 w_core(index, part, step).wait_recv()
 
-    def fill(slot, value):
+    def fill(slot, value, start=0):
         rows = value.shape[0]
         column = lax.rem(lax.broadcasted_iota(jnp.int32, (rows, channels), 0), width)
         wide = value.astype(jnp.float32)
         left = jnp.where(column == 0, 0.0, pltpu.roll(wide, 1, 0))
         right = jnp.where(column == width - 1, 0.0, pltpu.roll(wide, rows - 1, 0))
-        stack[slot, 0:rows, 0:channels] = left.astype(jnp.bfloat16)
-        stack[slot, 0:rows, channels:2 * channels] = value
-        stack[slot, 0:rows, 2 * channels:triple] = right.astype(jnp.bfloat16)
+        stack[slot, start:start + rows, 0:channels] = left.astype(jnp.bfloat16)
+        stack[slot, start:start + rows, channels:2 * channels] = value
+        stack[slot, start:start + rows, 2 * channels:triple] = right.astype(jnp.bfloat16)
 
     def conv(slot, weight, rows):
         result = None
@@ -220,7 +240,6 @@
             return wts.at[self.which, index]
 
         def advance_first(self):
-            fill(ACT_Q, act(fields[self.tick, FWD2]))
             out1 = trim(self.field(FWD1, grown).astype(jnp.float32) + conv(ACT_Q, self.weight(F), first_pixels))
             self.put(FWD1, out1[kept])
             fill(ACT_OUT, act(out1))
@@ -229,11 +248,14 @@
             out2 = self.field(FWD2).astype(jnp.float32) + conv(ACT_OUT, self.weight(G), pixels)
             self.put(FWD2, out2.astype(jnp.bfloat16))
 
-        def fill_returning(self):
-            fill(ACT_Y, act(fields[self.tick, RET1]))
-
-        def fill_grad(self):
-            fill(GRAD2, fields[self.tick, GRD2])
+        def fill_inner(self, slot):
+            value = self.field(TAKES[slot])
+            fill(slot, value if slot == GRAD2 else act(value), margin)
+
+        def fill_margins(self, slot):
+            for start in (0, margin + pixels):
+                value = fields[self.tick, TAKES[slot], start:start + margin]
+                fill(slot, value if slot == GRAD2 else act(value), start)
 
         def invert_second(self):
             q2 = trim(self.field(RET2, grown).astype(jnp.float32) - conv(ACT_Y, self.weight(G), first_pixels))
@@ -316,87 +338,102 @@
             send_sem=pair_send.at[which, index, target], recv_sem=pair_recv.at[which, index, target],
             device_id=(seg, core_band), device_id_type=MESH)
 
-    def reduce_copy(which, index, step):
-        return pltpu.make_async_remote_copy(
-            src_ref=reduced.at[which, index, step - 1], dst_ref=partial.at[which, index, step - 1],
-            send_sem=red_send.at[which, index, step - 1], recv_sem=red_recv.at[which, index, step - 1],
+    def reduce_copy(which, index, part, step):
+        rows = pl.ds(part * piece, piece)
+        return pltpu.make_async_remote_copy(
+            src_ref=reduced.at[which, index, step - 1, rows], dst_ref=partial.at[which, index, step - 1, rows],
+            send_sem=red_send.at[which, index, part, step - 1], recv_sem=red_recv.at[which, index, part, step - 1],
             device_id=(seg, 2 * lax.rem(group + step, groups) + core), device_id_type=MESH)
 
-    def ship_copy(index):
-        return pltpu.make_async_remote_copy(
-            src_ref=ship_src.at[index], dst_ref=ship_dst.at[index],
-            send_sem=ship_send.at[index], recv_sem=ship_recv.at[index],
+    def ship_copy(index, part):
+        rows = pl.ds(part * piece, piece)
+        return pltpu.make_async_remote_copy(
+            src_ref=ship_src.at[index, rows], dst_ref=ship_dst.at[index, rows],
+            send_sem=ship_send.at[index, part], recv_sem=ship_recv.at[index, part],
             device_id=(other_seg, band), device_id_type=MESH)
 
     def start_sums(which, index):
         for target in range(groups):
             pair_copy(which, index, target).start()
 
-    def pair_sum(which, index, target):
-        return total[which, index, chunk_rows(2 * target + core)] + paired[which, index, target].astype(jnp.float32)
+    def pair_sum(which, index, target, part):
+        rows = pl.ds(part * piece, piece)
+        return (total[which, index, w_rows(2 * target + core, part)]
+                + paired[which, index, target, rows].astype(jnp.float32))
 
     def pass_sums(which, index):
         for target in range(groups):
             pair_copy(which, index, target).wait_recv()
+        for part in range(pieces):
+            rows = pl.ds(part * piece, piece)
+            for step in range(1, groups):
+                value = pair_sum(which, index, lax.rem(group + step, groups), part)
+                reduced[which, index, step - 1, rows] = value.astype(jnp.bfloat16)
+                reduce_copy(which, index, part, step).start()
+
+    def finish_sums(which, index, part):
+        value = pair_sum(which, index, group, part)
         for step in range(1, groups):
-            reduced[which, index, step - 1] = pair_sum(which, index, lax.rem(group + step, groups)).astype(jnp.bfloat16)
-            reduce_copy(which, index, step).start()
-
-    def finish_sums(which, index):
-        value = pair_sum(which, index, group)
-        for step in range(1, groups):
-            reduce_copy(which, index, step).wait_recv()
-            value = value + partial[which, index, step - 1].astype(jnp.float32)
+            reduce_copy(which, index, part, step).wait_recv()
+            value = value + partial[which, index, step - 1, pl.ds(part * piece, piece)].astype(jnp.float32)
         return value
 
     def keep_sums(index):
-        owned[index] = finish_sums(OWN, index)
+        for part in range(pieces):
+            owned[index, pl.ds(part * piece, piece)] = finish_sums(OWN, index, part)
 
     def ship_sums(index):
-        ship_src[index] = finish_sums(OTHER, index).astype(jnp.bfloat16)
-        ship_copy(index).start()
+        for part in range(pieces):
+            ship_src[index, pl.ds(part * piece, piece)] = finish_sums(OTHER, index, part).astype(jnp.bfloat16)
+            ship_copy(index, part).start()
 
     def close_sums(index):
-        ship_copy(index).wait_recv()
-        wgrad_out[index] = owned[index] + ship_dst[index].astype(jnp.float32)
+        for part in range(pieces):
+            rows = pl.ds(part * piece, piece)
+            ship_copy(index, part).wait_recv()
+            wgrad_out[index, rows] = owned[index, rows] + ship_dst[index, rows].astype(jnp.float32)
 
     first = Tick(0, OWN, put_mid, lambda field: sent[0, field])
     load(RET1).wait()
+    first.fill_inner(ACT_Y)
     load(GRD2).wait()
-    load_weights(G).wait()
+    first.fill_inner(GRAD2)
+    load(FWD2).wait()
+    first.fill_inner(ACT_Q)
     load(RET2).wait()
     load(GRD1).wait()
+    load(FWD1).wait()
+    load_weights(G).wait()
     load_weights(F).wait()
-    load(FWD2).wait()
-    load(FWD1).wait()
     neighbours = below.astype(jnp.int32) + above.astype(jnp.int32)
     pl.semaphore_wait(barrier, bands + neighbours)
-    for field in (RET1, GRD2, RET2, GRD1, FWD2, FWD1):
+    for field in (RET1, RET2, GRD2, GRD1, FWD2, FWD1):
         send_halo(0, field)
-    for index in (G, F):
-        for part in range(pieces):
-            w_across(index, part).start()
+    start_weights(G)
+    start_weights(F)
 
     take_halo(0, RET1)
-    first.fill_returning()
+    first.fill_margins(ACT_Y)
     take_halo(0, RET2)
     first.invert_second()
     take_halo(0, GRD2)
-    first.fill_grad()
+    first.fill_margins(GRAD2)
     take_halo(0, GRD1)
     first.back_first()
+    spread_weights(G, 0)
     first.invert_first()
     first.back_second()
     send_mid(GRD1)
 
     @pl.when(odd)
     def _():
-        for field in (RET1, GRD2, RET2, GRD1):
+        for field in (RET1, RET2, GRD2, GRD1):
             send_halo(1, field)
 
-    for part in range(pieces - 1):
+    for part in range(1, pieces):
         spread_weights(G, part)
     take_halo(0, FWD2)
+    first.fill_margins(ACT_Q)
     take_halo(0, FWD1)
     first.advance_first()
     first.advance_second()
@@ -406,15 +443,13 @@
         for field in (FWD2, FWD1):
             send_halo(1, field)
 
-    spread_weights(G, pieces - 1)
     first.correlate_g()
     start_sums(OWN, G)
+    for part in range(pieces):
+        pass_weights(G, part)
     first.correlate_f()
     start_sums(OWN, F)
-    for part in range(pieces):
-        pass_weights(G, part)
-    for part in range(pieces - 1):
-        spread_weights(F, part)
+    pass_sums(OWN, G)
 
     @pl.when(odd)
     def _():
@@ -426,10 +461,12 @@
                 pl.when(end_back)(end_move(field).start)
 
         last = Tick(1, OTHER, put, lambda field: sent[1, field])
+        last.fill_inner(ACT_Y)
+        last.fill_inner(GRAD2)
         take_halo(1, RET1)
-        last.fill_returning()
+        last.fill_margins(ACT_Y)
         take_halo(1, GRD2)
-        last.fill_grad()
+        last.fill_margins(GRAD2)
         take_halo(1, RET2)
         take_halo(1, GRD1)
         take_weights(G)
@@ -437,31 +474,32 @@
         last.back_first()
         last.correlate_g()
         start_sums(OTHER, G)
+        for part in range(pieces):
+            spread_weights(F, part)
         last.correlate_f()
         start_sums(OTHER, F)
-        spread_weights(F, pieces - 1)
+        pass_sums(OTHER, G)
         for part in range(pieces):
             pass_weights(F, part)
-        pass_sums(OTHER, G)
         pass_sums(OTHER, F)
         take_weights(F)
         last.invert_first()
         last.back_second()
-        pass_sums(OWN, G)
         pass_sums(OWN, F)
-
         for field in (FWD2, FWD1):
             pl.when(below)(mid_move(field).wait_recv)
         pl.when(seg == 1)(edge(0).wait)
         for field in (FWD2, FWD1):
             send_halo(1, field)
+        last.fill_inner(ACT_Q)
+        keep_sums(G)
+        ship_sums(G)
         for field in (FWD2, FWD1):
             take_halo(1, field)
+        last.fill_margins(ACT_Q)
         last.advance_first()
         last.advance_second()
-        ship_sums(G)
         ship_sums(F)
-        keep_sums(G)
         keep_sums(F)
 
     @pl.when(even)
@@ -475,17 +513,6 @@
                 (ret_out, grd_out)[field // 2 - 1][field % 2] = value
 
         last = Tick(1, OTHER, put, lambda field: (ret_out, grd_out)[field // 2 - 1][field % 2])
-        spread_weights(F, pieces - 1)
-        for part in range(pieces):
-            pass_weights(F, part)
-        pass_sums(OWN, G)
-        pass_sums(OWN, F)
-        take_weights(F)
-        take_weights(G)
-        for field in (FWD2, FWD1):
-            take_halo(1, field)
-        last.advance_first()
-        last.advance_second()
 
         def arrive(field):
             if field < GRD1:
@@ -496,28 +523,43 @@
                     pl.when(leaves)(edge(2).wait)
             send_halo(1, field)
 
+        for part in range(pieces):
+            spread_weights(F, part)
+        last.fill_inner(ACT_Q)
         arrive(RET2)
         arrive(RET1)
+        last.fill_inner(ACT_Y)
+        pass_sums(OWN, F)
+        for part in range(pieces):
+            pass_weights(F, part)
+        take_weights(G)
         take_halo(1, RET1)
-        last.fill_returning()
+        last.fill_margins(ACT_Y)
         take_halo(1, RET2)
         last.invert_second()
+        for field in (FWD2, FWD1):
+            take_halo(1, field)
+        last.fill_margins(ACT_Q)
+        take_weights(F)
+        last.advance_first()
         arrive(GRD2)
-        keep_sums(G)
-        keep_sums(F)
-        take_halo(1, GRD2)
+        last.advance_second()
         last.correlate_g()
         start_sums(OTHER, G)
-        last.fill_grad()
+        last.fill_inner(GRAD2)
+        take_halo(1, GRD2)
+        last.fill_margins(GRAD2)
         arrive(GRD1)
+        pass_sums(OTHER, G)
+        last.invert_first()
         take_halo(1, GRD1)
-        pass_sums(OTHER, G)
         last.back_first()
         last.correlate_f()
         start_sums(OTHER, F)
-        last.invert_first()
+        last.back_second()
         pass_sums(OTHER, F)
-        last.back_second()
+        keep_sums(G)
+        keep_sums(F)
         ship_sums(G)
         ship_sums(F)
 
@@ -554,9 +596,11 @@
         for which in range(2):
             for target in range(groups):
                 pair_copy(which, index, target).wait_send()
-            for step in range(1, groups):
-                reduce_copy(which, index, step).wait_send()
-        ship_copy(index).wait_send()
+            for part in range(pieces):
+                for step in range(1, groups):
+                    reduce_copy(which, index, part, step).wait_send()
+        for part in range(pieces):
+            ship_copy(index, part).wait_send()
 
 
 def store(*refs):
@@ -623,10 +667,10 @@
             dma((2, pieces, groups)),
             dma((2, 2, groups)),
             dma((2, 2, groups)),
-            dma((2, 2, groups - 1)),
-            dma((2, 2, groups - 1)),
-            dma((2,)),
-            dma((2,)),
+            dma((2, 2, pieces, groups - 1)),
+            dma((2, 2, pieces, groups - 1)),
+            dma((2, pieces)),
+            dma((2, pieces)),
         ],
         compiler_params=pltpu.CompilerParams(
             collective_id=0, has_side_effects=True, vmem_limit_bytes=60 * 2**20),

time: 81.5 us -> 70.2 us (0.86)
  the two profiles are of different devices: /device:TPU:1 before, /device:TPU:28 now
where the time goes in v2:
time: 70.2 us; the launch traced here: 70.1 us
  Pallas kernels  69.3 us (99%)
  between operations  0.82 us (1%)
    pallas_call x1, Pallas kernels, local(): pl.pallas_call(functools.partial(kernel, segments, bands, width, pieces),...  66.4 us
    pallas_call x1, Pallas kernels, local(): pl.pallas_call(store, out_shape=tuple((jax.ShapeDtypeStruct(o.shape, o.dt...  2.84 us

profile of v2, /device:TPU:28, one launch (start us, length us, event | category | flops | bytes accessed | tf_op | source)
XLA Modules:
  0.0 70.1 jit_solution(8747892414553069028)
XLA Ops:
  0.6 66.4 %shard_map.93 = (bf16[2,512,256]{2,1,0:T(8,128)(2,1)}, bf16[2,512,256]{2,1,0:T(8,128)(2,1)}, bf16[2,512,256]{2,1,0:T(8,128)(2,1)}, f32[2,576,256]{2,1,0:T(8,128)}) custom-call(bf16[2,512,256]{2,1,0:T(8,128)(2,1)} %bitcast.13, bf16[2,512,256]{2,1,0:T(8,128)(2,1)} %bitcast.14, bf16[2,512,256]{2,1,0:T(8,128)(2,1)} %bitcast.15, bf16[2,2304,256]{2,1,0:T(8,128)(2,1)} %bitcast.10, ...), custom_call_target="tpu_custom_call" | custom-call | tf_op jit(solution)/shard_map/pallas_call | solution.py:635
  67.1 2.8 %shard_map.94 = (bf16[2,512,256]{2,1,0:T(8,128)(2,1)}, bf16[2,512,256]{2,1,0:T(8,128)(2,1)}, bf16[2,512,256]{2,1,0:T(8,128)(2,1)}, f32[2,576,256]{2,1,0:T(8,128)}) custom-call(bf16[2,512,256]{2,1,0:T(8,128)(2,1)} %get-tuple-element.12.refs_0_, bf16[2,512,256]{2,1,0:T(8,128)(2,1)} %get-tuple-element.13.refs_1_, ...), custom_call_target="tpu_custom_call" | custom-call | tf_op jit(solution)/shard_map/pallas_call | solution.py:679

commit v3 on v2

--- a/solution.py
+++ b/solution.py
@@ -18,7 +18,7 @@
 
 def kernel(segments, bands, width, pieces, fwd_in, ret_in, grd_in, weights_in, fresh_in, loss_in,
            fwd_out, ret_out, grd_out, wgrad_out,
-           fields, wts, stack, sent, total, total_half, paired, reduced, partial, owned, ship_src, ship_dst,
+           fields, wts, stack, sent, pulled, total, total_half, paired, reduced, partial, owned, ship_src, ship_dst,
            in_sem, w_sem, edge_sem, halo_send, halo_recv, mid_send, mid_recv, end_send, end_recv,
            wy_send, wy_recv, wx_send, wx_recv, wc_send, wc_recv,
            pair_send, pair_recv, red_send, red_recv, ship_send, ship_recv):
@@ -145,20 +145,20 @@
 
     straight = jnp.logical_and(above, other_seg < segments - 2) if groups == 2 else jnp.bool_(False)
 
+    def is_direct(index):
+        return straight if index == F else jnp.bool_(False)
+
     def start_weights(index):
         for part in range(pieces):
             w_across(index, part).start()
-            if index == F:
-                for step in range(1, groups):
-                    pl.when(straight)(w_direct(index, part, step).start)
+            for step in range(1, groups):
+                if index == F:
+                    pl.when(is_direct(index))(w_direct(index, part, step).start)
 
     def spread_weights(index, part):
         w_across(index, part).wait_recv()
         for step in range(1, groups):
-            if index == F:
-                pl.when(jnp.logical_not(straight))(w_group(index, part, step).start)
-            else:
-                w_group(index, part, step).start()
+            pl.when(jnp.logical_not(is_direct(index)))(w_group(index, part, step).start)
         w_core(index, part, 0).start()
 
     def pass_weights(index, part):
@@ -263,10 +263,18 @@
             fill(ACT_IN, act(q2))
 
         def back_first(self):
-            h1 = trim(self.field(GRD1, grown).astype(jnp.float32)
-                      + slope(self.field(RET1, grown)) * back(GRAD2, self.weight(G), first_pixels))
-            self.put(GRD1, h1[kept])
-            fill(BACK1, h1)
+            pulled[...] = slope(self.field(RET1, grown)) * back(GRAD2, self.weight(G), first_pixels)
+
+        def back_inner(self):
+            h1 = (self.field(GRD1).astype(jnp.float32) + pulled[kept]).astype(jnp.bfloat16)
+            self.put(GRD1, h1)
+            fill(BACK1, h1, width)
+
+        def back_margins(self):
+            for start, outside in ((0, at_top), (width + pixels, at_bottom)):
+                rows = slice(start, start + width)
+                grad = fields[self.tick, GRD1, start + width:start + 2 * width].astype(jnp.float32)
+                fill(BACK1, jnp.where(outside, 0.0, grad + pulled[rows]).astype(jnp.bfloat16), start)
 
         def invert_first(self):
             p2 = self.field(RET1).astype(jnp.float32) - conv(ACT_IN, self.weight(F), pixels)
@@ -418,8 +426,10 @@
     first.invert_second()
     take_halo(0, GRD2)
     first.fill_margins(GRAD2)
+    first.back_first()
     take_halo(0, GRD1)
-    first.back_first()
+    first.back_inner()
+    first.back_margins()
     spread_weights(G, 0)
     first.invert_first()
     first.back_second()
@@ -430,12 +440,34 @@
         for field in (RET1, RET2, GRD2, GRD1):
             send_halo(1, field)
 
+    first.correlate_g()
+    start_sums(OWN, G)
     for part in range(1, pieces):
         spread_weights(G, part)
+    first.correlate_f()
+    start_sums(OWN, F)
+    shared = jnp.logical_not(straight)
+
+    @pl.when(shared)
+    def _():
+        spread_weights(F, 0)
+
     take_halo(0, FWD2)
     first.fill_margins(ACT_Q)
     take_halo(0, FWD1)
     first.advance_first()
+
+    @pl.when(shared)
+    def _():
+        for part in range(1, pieces):
+            spread_weights(F, part)
+
+    @pl.when(straight)
+    def _():
+        pass_sums(OWN, G)
+
+    for part in range(pieces):
+        pass_weights(G, part)
     first.advance_second()
 
     @pl.when(even)
@@ -443,13 +475,9 @@
         for field in (FWD2, FWD1):
             send_halo(1, field)
 
-    first.correlate_g()
-    start_sums(OWN, G)
-    for part in range(pieces):
-        pass_weights(G, part)
-    first.correlate_f()
-    start_sums(OWN, F)
-    pass_sums(OWN, G)
+    @pl.when(shared)
+    def _():
+        pass_sums(OWN, G)
 
     @pl.when(odd)
     def _():
@@ -467,38 +495,45 @@
         last.fill_margins(ACT_Y)
         take_halo(1, GRD2)
         last.fill_margins(GRAD2)
+        last.correlate_g()
+        start_sums(OTHER, G)
         take_halo(1, RET2)
         take_halo(1, GRD1)
         take_weights(G)
         last.invert_second()
         last.back_first()
-        last.correlate_g()
-        start_sums(OTHER, G)
-        for part in range(pieces):
-            spread_weights(F, part)
+        last.back_inner()
+        last.back_margins()
+        pass_sums(OTHER, G)
         last.correlate_f()
         start_sums(OTHER, F)
-        pass_sums(OTHER, G)
-        for part in range(pieces):
-            pass_weights(F, part)
-        pass_sums(OTHER, F)
-        take_weights(F)
-        last.invert_first()
-        last.back_second()
-        pass_sums(OWN, F)
+
+        @pl.when(straight)
+        def _():
+            for part in range(pieces):
+                spread_weights(F, part)
+
         for field in (FWD2, FWD1):
             pl.when(below)(mid_move(field).wait_recv)
         pl.when(seg == 1)(edge(0).wait)
         for field in (FWD2, FWD1):
             send_halo(1, field)
+        for part in range(pieces):
+            pass_weights(F, part)
+        pass_sums(OTHER, F)
+        pass_sums(OWN, F)
+
+        take_weights(F)
+        last.invert_first()
+        last.back_second()
         last.fill_inner(ACT_Q)
-        keep_sums(G)
         ship_sums(G)
         for field in (FWD2, FWD1):
             take_halo(1, field)
         last.fill_margins(ACT_Q)
         last.advance_first()
         last.advance_second()
+        keep_sums(G)
         ship_sums(F)
         keep_sums(F)
 
@@ -523,48 +558,87 @@
                     pl.when(leaves)(edge(2).wait)
             send_halo(1, field)
 
-        for part in range(pieces):
-            spread_weights(F, part)
-        last.fill_inner(ACT_Q)
-        arrive(RET2)
-        arrive(RET1)
-        last.fill_inner(ACT_Y)
+        @pl.when(straight)
+        def _():
+            arrive(RET2)
+            arrive(RET1)
+            last.fill_inner(ACT_Y)
+            last.fill_inner(ACT_Q)
+            for field in (FWD2, FWD1):
+                take_halo(1, field)
+            last.fill_margins(ACT_Q)
+            take_halo(1, RET1)
+            last.fill_margins(ACT_Y)
+            take_weights(G)
+            take_halo(1, RET2)
+            last.invert_second()
+            for part in range(pieces):
+                spread_weights(F, part)
+            arrive(GRD2)
+            last.correlate_g()
+            start_sums(OTHER, G)
+            for part in range(pieces):
+                pass_weights(F, part)
+            take_weights(F)
+            last.advance_first()
+            last.fill_inner(GRAD2)
+            take_halo(1, GRD2)
+            last.fill_margins(GRAD2)
+            pass_sums(OTHER, G)
+            last.back_first()
+            arrive(GRD1)
+            last.back_inner()
+            last.correlate_f()
+            start_sums(OTHER, F)
+            last.advance_second()
+
+        @pl.when(shared)
+        def _():
+            arrive(GRD2)
+            arrive(GRD1)
+            last.fill_inner(GRAD2)
+            last.fill_inner(ACT_Q)
+            for part in range(pieces):
+                pass_weights(F, part)
+            for field in (FWD2, FWD1):
+                take_halo(1, field)
+            last.fill_margins(ACT_Q)
+            take_weights(G)
+            take_weights(F)
+            last.advance_first()
+            last.advance_second()
+            arrive(RET1)
+            last.fill_inner(ACT_Y)
+            take_halo(1, RET1)
+            last.fill_margins(ACT_Y)
+            last.correlate_g()
+            start_sums(OTHER, G)
+            take_halo(1, GRD2)
+            last.fill_margins(GRAD2)
+            last.back_first()
+            last.back_inner()
+            arrive(RET2)
+            pass_sums(OTHER, G)
+            take_halo(1, RET2)
+            last.invert_second()
+            last.correlate_f()
+            start_sums(OTHER, F)
+            last.invert_first()
+
+        pass_sums(OTHER, F)
         pass_sums(OWN, F)
-        for part in range(pieces):
-            pass_weights(F, part)
-        take_weights(G)
-        take_halo(1, RET1)
-        last.fill_margins(ACT_Y)
-        take_halo(1, RET2)
-        last.invert_second()
-        for field in (FWD2, FWD1):
-            take_halo(1, field)
-        last.fill_margins(ACT_Q)
-        take_weights(F)
-        last.advance_first()
-        arrive(GRD2)
-        last.advance_second()
-        last.correlate_g()
-        start_sums(OTHER, G)
-        last.fill_inner(GRAD2)
-        take_halo(1, GRD2)
-        last.fill_margins(GRAD2)
-        arrive(GRD1)
-        pass_sums(OTHER, G)
-        last.invert_first()
+
+        @pl.when(straight)
+        def _():
+            last.invert_first()
+
         take_halo(1, GRD1)
-        last.back_first()
-        last.correlate_f()
-        start_sums(OTHER, F)
+        last.back_margins()
         last.back_second()
-        pass_sums(OTHER, F)
         keep_sums(G)
-        keep_sums(F)
         ship_sums(G)
         ship_sums(F)
-
-    close_sums(G)
-    close_sums(F)
+        keep_sums(F)
 
     pl.when(first_seg)(edge(1).wait)
     pl.when(last_seg)(edge(3).wait)
@@ -599,6 +673,10 @@
             for part in range(pieces):
                 for step in range(1, groups):
                     reduce_copy(which, index, part, step).wait_send()
+
+    close_sums(G)
+    close_sums(F)
+    for index in range(2):
         for part in range(pieces):
             ship_copy(index, part).wait_send()
 
@@ -625,7 +703,7 @@
     taps = weights.shape[2]
     chunk = taps // bands
     groups = bands // 2
-    pieces = 2 if chunk % 32 == 0 else 1
+    pieces = next(count for count in (2, 1) if chunk % (16 * count) == 0 or count == 1)
     assert fresh_input.shape[0] == 2 and segments % 2 == 0 and bands % 2 == 0 and rows >= 2
     bf16, f32 = jnp.bfloat16, jnp.float32
     pair = jax.ShapeDtypeStruct((2, pixels, channels), bf16)
@@ -642,6 +720,7 @@
             pltpu.VMEM((2, 2, taps, channels), bf16),
             pltpu.VMEM((6, pixels + 4 * width, 3 * channels), bf16),
             pltpu.VMEM((2, 6, pixels, channels), bf16),
+            pltpu.VMEM((pixels + 2 * width, channels), f32),
             pltpu.VMEM((2, 2, taps, channels), f32),
             pltpu.VMEM((2, 2, taps, channels), bf16),
             pltpu.VMEM((2, 2, groups, chunk, channels), bf16),

time: 70.2 us -> 65.5 us (0.933)
  Pallas kernels: 69.3 us -> 64.5 us
    pallas_call x1, Pallas kernels: 66.4 us -> 61.7 us  [local(): pl.pallas_call(functools.partial(kernel, segments, bands, width, pieces),...]
where the time goes in v3:
time: 65.5 us; the launch traced here: 65.3 us
  Pallas kernels  64.5 us (98%)
  between operations  0.84 us (1%)
    pallas_call x1, Pallas kernels, local(): pl.pallas_call(functools.partial(kernel, segments, bands, width, pieces),...  61.7 us
    pallas_call x1, Pallas kernels, local(): pl.pallas_call(store, out_shape=tuple((jax.ShapeDtypeStruct(o.shape, o.dt...  2.84 us

profile of v3, /device:TPU:28, one launch (start us, length us, event | category | flops | bytes accessed | tf_op | source)
XLA Modules:
  0.0 65.3 jit_solution(1957624431609572106)
XLA Ops:
  0.6 61.7 %shard_map.93 = (bf16[2,512,256]{2,1,0:T(8,128)(2,1)}, bf16[2,512,256]{2,1,0:T(8,128)(2,1)}, bf16[2,512,256]{2,1,0:T(8,128)(2,1)}, f32[2,576,256]{2,1,0:T(8,128)}) custom-call(bf16[2,512,256]{2,1,0:T(8,128)(2,1)} %bitcast.13, bf16[2,512,256]{2,1,0:T(8,128)(2,1)} %bitcast.14, bf16[2,512,256]{2,1,0:T(8,128)(2,1)} %bitcast.15, bf16[2,2304,256]{2,1,0:T(8,128)(2,1)} %bitcast.10, ...), custom_call_target="tpu_custom_call" | custom-call | tf_op jit(solution)/shard_map/pallas_call | solution.py:713
  62.3 2.8 %shard_map.94 = (bf16[2,512,256]{2,1,0:T(8,128)(2,1)}, bf16[2,512,256]{2,1,0:T(8,128)(2,1)}, bf16[2,512,256]{2,1,0:T(8,128)(2,1)}, f32[2,576,256]{2,1,0:T(8,128)}) custom-call(bf16[2,512,256]{2,1,0:T(8,128)(2,1)} %get-tuple-element.12.refs_0_, bf16[2,512,256]{2,1,0:T(8,128)(2,1)} %get-tuple-element.13.refs_1_, ...), custom_call_target="tpu_custom_call" | custom-call | tf_op jit(solution)/shard_map/pallas_call | solution.py:758

commit v4 on v3

--- a/solution.py
+++ b/solution.py
@@ -369,10 +369,13 @@
         return (total[which, index, w_rows(2 * target + core, part)]
                 + paired[which, index, target, rows].astype(jnp.float32))
 
-    def pass_sums(which, index):
-        for target in range(groups):
-            pair_copy(which, index, target).wait_recv()
-        for part in range(pieces):
+    early, late = range((pieces + 1) // 2), range((pieces + 1) // 2, pieces)
+
+    def pass_sums(which, index, parts=range(pieces)):
+        if 0 in parts:
+            for target in range(groups):
+                pair_copy(which, index, target).wait_recv()
+        for part in parts:
             rows = pl.ds(part * piece, piece)
             for step in range(1, groups):
                 value = pair_sum(which, index, lax.rem(group + step, groups), part)
@@ -448,6 +451,10 @@
     start_sums(OWN, F)
     shared = jnp.logical_not(straight)
 
+    @pl.when(jnp.logical_and(straight, even))
+    def _():
+        pass_sums(OWN, G, early)
+
     @pl.when(shared)
     def _():
         spread_weights(F, 0)
@@ -462,9 +469,10 @@
         for part in range(1, pieces):
             spread_weights(F, part)
 
-    @pl.when(straight)
+    @pl.when(jnp.logical_and(straight, odd))
     def _():
         pass_sums(OWN, G)
+        pass_sums(OWN, F)
 
     for part in range(pieces):
         pass_weights(G, part)
@@ -521,7 +529,11 @@
         for part in range(pieces):
             pass_weights(F, part)
         pass_sums(OTHER, F)
-        pass_sums(OWN, F)
+
+        @pl.when(shared)
+        def _():
+            pass_sums(OWN, F)
+
 
         take_weights(F)
         last.invert_first()
@@ -567,6 +579,8 @@
             for field in (FWD2, FWD1):
                 take_halo(1, field)
             last.fill_margins(ACT_Q)
+            pass_sums(OWN, G, late)
+            pass_sums(OWN, F, early)
             take_halo(1, RET1)
             last.fill_margins(ACT_Y)
             take_weights(G)
@@ -575,6 +589,7 @@
             for part in range(pieces):
                 spread_weights(F, part)
             arrive(GRD2)
+            pass_sums(OWN, F, late)
             last.correlate_g()
             start_sums(OTHER, G)
             for part in range(pieces):
@@ -606,19 +621,20 @@
             take_weights(G)
             take_weights(F)
             last.advance_first()
-            last.advance_second()
             arrive(RET1)
             last.fill_inner(ACT_Y)
+            last.advance_second()
             take_halo(1, RET1)
             last.fill_margins(ACT_Y)
             last.correlate_g()
             start_sums(OTHER, G)
+            arrive(RET2)
             take_halo(1, GRD2)
             last.fill_margins(GRAD2)
+            pass_sums(OWN, F, early)
+            pass_sums(OTHER, G)
             last.back_first()
             last.back_inner()
-            arrive(RET2)
-            pass_sums(OTHER, G)
             take_halo(1, RET2)
             last.invert_second()
             last.correlate_f()
@@ -626,7 +642,11 @@
             last.invert_first()
 
         pass_sums(OTHER, F)
-        pass_sums(OWN, F)
+
+        @pl.when(shared)
+        def _():
+            pass_sums(OWN, F, late)
+
 
         @pl.when(straight)
         def _():
@@ -685,8 +705,9 @@
     count = (len(refs) - 2) // 3
     sources, targets, held = refs[:count], refs[count:2 * count], refs[2 * count:3 * count]
     load_sem, store_sem = refs[3 * count:]
-    loads = [pltpu.make_async_copy(sources[i], held[i], load_sem.at[i]) for i in range(count)]
-    stores = [pltpu.make_async_copy(held[i], targets[i], store_sem.at[i]) for i in range(count)]
+    parts = [(i, j) for i in reversed(range(count)) for j in range(held[i].shape[0])]
+    loads = [pltpu.make_async_copy(sources[i].at[j], held[i].at[j], load_sem.at[i, j]) for i, j in parts]
+    stores = [pltpu.make_async_copy(held[i].at[j], targets[i].at[j], store_sem.at[i, j]) for i, j in parts]
     for load in loads:
         load.start()
     for load, out in zip(loads, stores):
@@ -760,7 +781,7 @@
         out_shape=tuple(jax.ShapeDtypeStruct(o.shape, o.dtype) for o in outs),
         in_specs=[pl.BlockSpec(memory_space=pl.ANY)] * 4,
         out_specs=(pl.BlockSpec(memory_space=pl.ANY),) * 4,
-        scratch_shapes=[pltpu.VMEM(o.shape, o.dtype) for o in outs] + [dma((4,)), dma((4,))],
+        scratch_shapes=[pltpu.VMEM(o.shape, o.dtype) for o in outs] + [dma((4, 2)), dma((4, 2))],
     )(*outs)
     shape = forward_state.shape
     return tuple(o.reshape(shape) for o in outs[:3]) + (outs[3][None],)

time: 65.5 us -> 64 us (0.977)
  Pallas kernels: 64.5 us -> 62.6 us
    pallas_call x1, Pallas kernels: 61.7 us -> 59.8 us  [local(): pl.pallas_call(functools.partial(kernel, segments, bands, width, pieces),...]
where the time goes in v4:
time: 64 us; the launch traced here: 63.4 us
  Pallas kernels  62.6 us (98%)
  between operations  0.86 us (1%)
    pallas_call x1, Pallas kernels, local(): pl.pallas_call(functools.partial(kernel, segments, bands, width, pieces),...  59.8 us
    pallas_call x1, Pallas kernels, local(): pl.pallas_call(store, out_shape=tuple((jax.ShapeDtypeStruct(o.shape, o.dt...  2.73 us

profile of v4, /device:TPU:28, one launch (start us, length us, event | category | flops | bytes accessed | tf_op | source)
XLA Modules:
  0.0 63.4 jit_solution(9019881917170895243)
XLA Ops:
  0.6 59.8 %shard_map.93 = (bf16[2,512,256]{2,1,0:T(8,128)(2,1)}, bf16[2,512,256]{2,1,0:T(8,128)(2,1)}, bf16[2,512,256]{2,1,0:T(8,128)(2,1)}, f32[2,576,256]{2,1,0:T(8,128)}) custom-call(bf16[2,512,256]{2,1,0:T(8,128)(2,1)} %bitcast.13, bf16[2,512,256]{2,1,0:T(8,128)(2,1)} %bitcast.14, bf16[2,512,256]{2,1,0:T(8,128)(2,1)} %bitcast.15, bf16[2,2304,256]{2,1,0:T(8,128)(2,1)} %bitcast.10, ...), custom_call_target="tpu_custom_call" | custom-call | tf_op jit(solution)/shard_map/pallas_call | solution.py:734
  60.5 2.7 %shard_map.94 = (bf16[2,512,256]{2,1,0:T(8,128)(2,1)}, bf16[2,512,256]{2,1,0:T(8,128)(2,1)}, bf16[2,512,256]{2,1,0:T(8,128)(2,1)}, f32[2,576,256]{2,1,0:T(8,128)}) custom-call(bf16[2,512,256]{2,1,0:T(8,128)(2,1)} %get-tuple-element.12.refs_0_, bf16[2,512,256]{2,1,0:T(8,128)(2,1)} %get-tuple-element.13.refs_1_, ...), custom_call_target="tpu_custom_call" | custom-call | tf_op jit(solution)/shard_map/pallas_call | solution.py:779

commit v5 on v4

--- a/solution.py
+++ b/solution.py
@@ -145,20 +145,23 @@
 
     straight = jnp.logical_and(above, other_seg < segments - 2) if groups == 2 else jnp.bool_(False)
 
-    def is_direct(index):
-        return straight if index == F else jnp.bool_(False)
+    def is_direct(index, part):
+        if index == G or groups != 2:
+            return jnp.bool_(False)
+        return jnp.bool_(True) if part < pieces // 2 else straight
 
     def start_weights(index):
         for part in range(pieces):
             w_across(index, part).start()
-            for step in range(1, groups):
-                if index == F:
-                    pl.when(is_direct(index))(w_direct(index, part, step).start)
+        if index == F:
+            for part in range(pieces):
+                for step in range(1, groups):
+                    pl.when(is_direct(index, part))(w_direct(index, part, step).start)
 
     def spread_weights(index, part):
         w_across(index, part).wait_recv()
         for step in range(1, groups):
-            pl.when(jnp.logical_not(is_direct(index)))(w_group(index, part, step).start)
+            pl.when(jnp.logical_not(is_direct(index, part)))(w_group(index, part, step).start)
         w_core(index, part, 0).start()
 
     def pass_weights(index, part):

time: 64 us -> 62.6 us (0.978)
  Pallas kernels: 62.6 us -> 61.4 us
    pallas_call x1, Pallas kernels: 59.8 us -> 58.7 us  [local(): pl.pallas_call(functools.partial(kernel, segments, bands, width, pieces),...]
where the time goes in v5:
time: 62.6 us; the launch traced here: 62.3 us
  Pallas kernels  61.4 us (98%)
  between operations  0.86 us (1%)
    pallas_call x1, Pallas kernels, local(): pl.pallas_call(functools.partial(kernel, segments, bands, width, pieces),...  58.7 us
    pallas_call x1, Pallas kernels, local(): pl.pallas_call(store, out_shape=tuple((jax.ShapeDtypeStruct(o.shape, o.dt...  2.73 us

profile of v5, /device:TPU:28, one launch (start us, length us, event | category | flops | bytes accessed | tf_op | source)
XLA Modules:
  0.0 62.3 jit_solution(5434652932186805945)
XLA Ops:
  0.6 58.7 %shard_map.93 = (bf16[2,512,256]{2,1,0:T(8,128)(2,1)}, bf16[2,512,256]{2,1,0:T(8,128)(2,1)}, bf16[2,512,256]{2,1,0:T(8,128)(2,1)}, f32[2,576,256]{2,1,0:T(8,128)}) custom-call(bf16[2,512,256]{2,1,0:T(8,128)(2,1)} %bitcast.13, bf16[2,512,256]{2,1,0:T(8,128)(2,1)} %bitcast.14, bf16[2,512,256]{2,1,0:T(8,128)(2,1)} %bitcast.15, bf16[2,2304,256]{2,1,0:T(8,128)(2,1)} %bitcast.10, ...), custom_call_target="tpu_custom_call" | custom-call | tf_op jit(solution)/shard_map/pallas_call | solution.py:737
  59.3 2.7 %shard_map.94 = (bf16[2,512,256]{2,1,0:T(8,128)(2,1)}, bf16[2,512,256]{2,1,0:T(8,128)(2,1)}, bf16[2,512,256]{2,1,0:T(8,128)(2,1)}, f32[2,576,256]{2,1,0:T(8,128)}) custom-call(bf16[2,512,256]{2,1,0:T(8,128)(2,1)} %get-tuple-element.12.refs_0_, bf16[2,512,256]{2,1,0:T(8,128)(2,1)} %get-tuple-element.13.refs_1_, ...), custom_call_target="tpu_custom_call" | custom-call | tf_op jit(solution)/shard_map/pallas_call | solution.py:782
